TPU v7x, 32 devices: a whole 2x2x4 slice. The times are simulated.
32 devices in a mesh: dp: 4 (over z), seq: 8 (over y, x, core).
Axes of the slice: x: 2, y: 2, z: 4, core: 2. Of those that a mesh axis runs over, the one named last changes fastest.
Arguments:
- layer_input: bfloat16 [4, 2048, 1024], P('dp', 'seq'), may hold values from -6 to 6
- w_qkv: bfloat16 [1024, 3072], replicated, may hold values from -8.75 to 8.75
- w_out: bfloat16 [1024, 1024], replicated, may hold values from -0.1875 to 0.1875
- w_proj: bfloat16 [16, 64, 256], replicated, may hold values from -35 to 35
- w_up: bfloat16 [1024, 4096], P('dp', 'seq'), may hold values from -0.1875 to 0.1875
- w_down: bfloat16 [1024, 4096], P('dp', 'seq'), may hold values from -0.09375 to 0.09375
Outputs:
- layer_output: bfloat16 [4, 2048, 1024], P('dp', 'seq')
All inputs are finite; a program needn't handle non-finite values.
Results may differ from a plain program's by a relative error of at most 0.025.
The roundings to bfloat16 on the way count: a program that leaves them out, or rounds other values in their place, can miss the bound.
Values may be sent and summed in bfloat16 or wider, within the bound.
No kernel may reach another device: no remote copies, remote signals or barrier semaphores. Data moves between devices by JAX's collectives and lax.ppermute only.
A program may use at most 128 MiB of HBM per device.

v0:
```python
import jax
import jax.numpy as jnp
from jax import lax
from jax.sharding import PartitionSpec as P

D = 1024
H = 16
HS = 64
WBLK = 256
epsilon = 1e-05


def extended_2(x, sides, width):
    for axis, dim in sides:
        peers, length = (lax.axis_size(axis), x.shape[dim])
        up = [(i, (i + 1) % peers) for i in range(peers - 1)]
        down = [(j, i) for i, j in up]
        last = lax.slice_in_dim(x, length - width, length, axis=dim)
        initial = lax.slice_in_dim(x, 0, width, axis=dim)
        before = lax.ppermute(last, axis, up)
        after = lax.ppermute(initial, axis, down)
        x = jnp.concatenate([before, x, after], axis=dim)
    return x


def normalize(value):
    center = value - jnp.mean(value, axis=-1, keepdims=True)
    spread = jnp.mean(center * center, axis=-1, keepdims=True)
    return center * lax.rsqrt(spread + epsilon)


def attend(block_query, near_keys, near_values, inside, far_keys, far_values):
    scale = HS ** (-0.5)
    near = (
        jnp.einsum("qhd,khd->hqk", block_query, near_keys, preferred_element_type=jnp.float32)
        * scale
    )
    near = jnp.where(inside[None, None, :], near, -jnp.inf)
    far = (
        jnp.einsum("qhd,hrd->hqr", block_query, far_keys, preferred_element_type=jnp.float32)
        * scale
    )
    weights = jax.nn.softmax(jnp.concatenate([near, far], axis=-1), axis=-1).astype(jnp.bfloat16)
    reach = near_keys.shape[0]
    mixed = jnp.einsum(
        "hqk,khd->qhd", weights[..., :reach], near_values, preferred_element_type=jnp.float32
    )
    mixed = mixed + jnp.einsum(
        "hqr,hrd->qhd", weights[..., reach:], far_values, preferred_element_type=jnp.float32
    )
    return mixed.astype(jnp.bfloat16).reshape(block_query.shape[0], H * HS)


def weighted_sums(exponent, paired):
    upper = exponent.astype(jnp.bfloat16)
    lower = (exponent - upper.astype(jnp.float32)).astype(jnp.bfloat16)
    sums = jnp.einsum("hnr,nhc->hrc", upper, paired, preferred_element_type=jnp.float32)
    return sums + jnp.einsum("hnr,nhc->hrc", lower, paired, preferred_element_type=jnp.float32)


def on_device(layer_input, w_qkv, w_out, w_proj, w_up, w_down):
    tokens = layer_input[0]
    rows = tokens.shape[0]
    normed = normalize(tokens.astype(jnp.float32)).astype(jnp.bfloat16)
    qkv = jnp.dot(normed, w_qkv, preferred_element_type=jnp.float32).astype(jnp.bfloat16)
    query = qkv[:, :D].reshape(rows, H, HS)
    keys = qkv[:, D : 2 * D].reshape(rows, H, HS)
    values = qkv[:, 2 * D :].reshape(rows, H, HS)
    paired = jnp.concatenate([keys, values], axis=-1)
    logits = jnp.einsum("nhd,hdr->hnr", keys, w_proj, preferred_element_type=jnp.float32)
    peaks = jnp.max(logits, axis=1)
    peaks = lax.pmax(peaks, "seq")
    exponent = jnp.exp(logits - peaks[:, None, :])
    totals = jnp.sum(exponent, axis=1)
    sums = weighted_sums(exponent, paired)
    totals, sums = (
        lax.psum(totals.astype(jnp.bfloat16), "seq").astype(jnp.float32),
        lax.psum(sums.astype(jnp.bfloat16), "seq").astype(jnp.float32),
    )
    summary = sums / totals[..., None]
    far_keys = normalize(summary[..., :HS]).astype(jnp.bfloat16)
    far_values = normalize(summary[..., HS:]).astype(jnp.bfloat16)
    local_pairs = normalize(paired.astype(jnp.float32).reshape(rows, H, 2, HS)).astype(jnp.bfloat16)
    local_pairs = local_pairs.reshape(rows, 2 * D)
    extended = extended_2(local_pairs, (("seq", 0),), WBLK)
    extended = extended.reshape(rows + 2 * WBLK, H, 2 * HS)
    first_place = lax.axis_index("seq") * rows
    length = rows * lax.axis_size("seq")
    offsets = jnp.arange(3 * WBLK, dtype=jnp.int32) - WBLK

    def per_block(which):
        start = which * WBLK
        places = first_place + start + offsets
        inside = (places >= 0) & (places < length)
        return attend(query, extended[..., :HS], extended[..., HS:], inside, far_keys, far_values)

    attn = lax.map(per_block, jnp.arange(rows // WBLK, dtype=jnp.int32)).reshape(rows, D)
    mixed = (
        tokens.astype(jnp.float32) + jnp.dot(attn, w_out, preferred_element_type=jnp.float32)
    ).astype(jnp.bfloat16)
    normed_two = normalize(mixed.astype(jnp.float32)).astype(jnp.bfloat16)
    up_part, down_part = (
        lax.all_gather(w_up, "dp", axis=0, tiled=True),
        lax.all_gather(w_down, "dp", axis=0, tiled=True),
    )
    hidden = jax.nn.gelu(
        jnp.dot(
            normed_two,
            lax.all_gather(up_part, "seq", axis=1, tiled=True),
            preferred_element_type=jnp.float32,
        )
    ).astype(jnp.bfloat16)
    feed = lax.dot_general(
        hidden,
        lax.all_gather(down_part, "seq", axis=1, tiled=True),
        (((1,), (1,)), ((), ())),
        preferred_element_type=jnp.float32,
    )
    result = (mixed.astype(jnp.float32) + feed).astype(jnp.bfloat16)
    return result[None]


def solution(mesh):
    in_specs = (P("dp", "seq", None), P(), P(), P(), P("dp", "seq"), P("dp", "seq"))
    out_specs = P("dp", "seq", None)
    return jax.shard_map(
        on_device, mesh=mesh, in_specs=in_specs, out_specs=out_specs, check_vma=False
    )
```

profile of v0, /device:TPU:0, one launch (start us, length us, event | category | flops | bytes accessed | tf_op | source)
XLA Modules:
  0.0 214.8 jit_solution(4927498811563739137)
XLA Ops:
  8.9 1.2 convert_reduce_fusion.2
  10.1 1.3 fusion.59
  11.4 4.9 %convolution_convert_fusion = bf16[256,3072]{1,0:T(8,128)(2,1)S(1)} fusion(bf16[1024,3072]{1,0:T(8,128)(2,1)} %param.7, bf16[1,256,1024]{2,1,0:T(8,128)(2,1)} %param.6, f32[256]{0:T(256)S(1)} %add_rsqrt_fusion.4, f32[256]{0:T(256)S(1)} %broadcast_multiply_fusion.4), kind=kOutput, calls=%fused_computation.18 | convolution fusion | flops 1612447744 | bytes 8390656 | tf_op jit(solution)/shard_map/dot_general | solution.py:65
  16.3 1.1 fusion.87
  17.6 1.2 copy.19
  18.8 1.4 copy.25
  20.2 1.3 copy.26
  21.5 3.7 %fusion.88 = (f32[16,256]{1,0:T(8,128)S(1)}, f32[16,256,256]{2,1,0:T(8,128)}) fusion(bf16[256,16,64]{0,2,1:T(8,128)(2,1)S(1)} %bitcast.41, bf16[16,64,256]{2,1,0:T(8,128)(2,1)} %param.9), kind=kOutput, calls=%fused_computation.104 | convolution fusion | flops 135262208 | bytes 5259264 | tf_op jit(solution)/shard_map/nhd,hdr->hnr/dot_general | solution.py:70
  25.3 26.3 %pmax.7 = f32[16,256]{1,0:T(8,128)S(1)} all-reduce(f32[16,256]{1,0:T(8,128)S(1)} %get-tuple-element.36), channel_id=1, replica_groups=mesh['dp'=4,'seq'=8] {'seq'}, use_global_device_ids=true, to_apply=%region_5.0 | all-reduce | flops 4096 | bytes 32768 | tf_op jit(solution)/shard_map/pmax | solution.py:72
  51.6 4.4 %fusion.14 = f32[16,256,128]{2,1,0:T(8,128)S(1)} fusion(f32[16,256,256]{2,1,0:T(8,128)} %get-tuple-element.37, f32[16,256]{1,0:T(8,128)S(1)} %pmax.7, bf16[256,16,64]{2,0,1:T(8,128)(2,1)} %copy.26, bf16[256,16,64]{2,0,1:T(8,128)(2,1)} %copy.25), kind=kOutput, calls=%fused_computation.22 | convolution fusion | flops 272629760 | bytes 7356416 | tf_op jit(solution)/shard_map/hnr,nhc->hrc/dot_general | solution.py:57
  56.3 2.7 %add_convert_fusion = bf16[16,256,128]{2,1,0:T(8,128)(2,1)} fusion(f32[16,256,128]{2,1,0:T(8,128)S(1)} %fusion.14, f32[16,256,256]{2,1,0:T(8,128)S(1)} %copy-done.1, f32[16,256]{1,0:T(8,128)S(1)} %pmax.7, bf16[256,16,64]{2,0,1:T(8,128)(2,1)S(1)} %copy-done.3, bf16[256,16,64]{2,0,1:T(8,128)(2,1)S(1)} %copy-done.2), kind=kOutput, calls=%fused_computation.43 | convolution fusion | flops 276824064 | bytes 8404992 | tf_op jit(solution)/shard_map/hnr,nhc->hrc/dot_general | solution.py:58
  59.8 9.7 %all-gather.5.cloned.1.call-done = bf16[1024,512]{1,0:T(8,128)(2,1)} async-done(((bf16[256,512]{1,0:T(8,128)(2,1)}), bf16[1024,512]{1,0:T(8,128)(2,1)}) %all-gather.5.cloned.1.call-update) | async-done | bytes 1048592 | tf_op jit(solution)/shard_map/all_gather | solution.py:103
  70.5 1.2 copy.20
  71.6 2.3 %collective-permute-start = (bf16[256,2048]{0,1:T(8,128)(2,1)}, bf16[256,2048]{0,1:T(8,128)(2,1)}, u32[]{:S(2)}, u32[]{:S(2)}) collective-permute-start(bf16[256,2048]{0,1:T(8,128)(2,1)} %bitcast.3), channel_id=1, source_target_pairs={{0,1},{1,2},{2,3},{3,4},{4,5},{5,6},{6,7},{8,9},{9,10},{10,11},{11... | collective-permute-start | bytes 3145736 | tf_op jit(solution)/shard_map/ppermute | solution.py:20
  73.9 1.3 collective-permute-start.1
  75.2 1.2 copy.22
  76.4 3.3 %fusion.12 = bf16[16,256]{1,0:T(8,128)(2,1)S(1)} fusion(f32[16,256,256]{2,1,0:T(8,128)} %get-tuple-element.37, f32[16,256]{1,0:T(8,128)S(1)} %pmax.7), kind=kLoop, calls=%fused_computation.19 | loop fusion | flops 2093056 | bytes 4218880 | tf_op jit(solution)/shard_map/reduce_sum | solution.py:74
  79.7 43.4 %psum.15 = bf16[16,256]{1,0:T(8,128)(2,1)S(1)} all-reduce(bf16[16,256]{1,0:T(8,128)(2,1)S(1)} %fusion.12), channel_id=1, replica_groups=mesh['dp'=4,'seq'=8] {'seq'}, use_global_device_ids=true, to_apply=%region_8.0 | all-reduce | flops 4096 | bytes 16384 | tf_op jit(solution)/shard_map/psum | solution.py:77
  123.2 40.4 %all-reduce.2.cloned.1.call-done = bf16[16,256,128]{2,1,0:T(8,128)(2,1)} async-done(((bf16[16,256,128]{2,1,0:T(8,128)(2,1)}), bf16[16,256,128]{2,1,0:T(8,128)(2,1)}) %all-reduce.2.cloned.1.call-update) | async-done | bytes 1048592 | tf_op jit(solution)/shard_map/psum | solution.py:78
  163.5 1.8 convert_divide_fusion
  165.3 1.7 slice_reduce_fusion
  167.0 2.9 %multiply_reduce_fusion = (f32[16,256]{1,0:T(8,128)S(1)}, f32[16,256]{1,0:T(8,128)S(1)}) fusion(f32[16,256,128]{2,1,0:T(8,128)S(1)} %convert_divide_fusion, f32[16,256]{1,0:T(8,128)S(1)} %broadcast_multiply_fusion.1, f32[16,256]{1,0:T(8,128)S(1)} %broadcast_multiply_fusion.2), kind=kLoop, calls=%fused_computation.39 | loop fusion | flops 1564672 | bytes 2162688 | tf_op jit(solution)/shard_map/reduce_sum | solution.py:28
  170.0 4.3 %fusion.90 = (f32[16,256]{1,0:T(8,128)S(1)}, f32[16,256,256]{2,1,0:T(8,128)S(1)}) fusion(bf16[256,16,64]{0,2,1:T(8,128)(2,1)S(1)} %bitcast.49, f32[16,256,128]{2,1,0:T(8,128)S(1)} %convert_divide_fusion, f32[16,256]{1,0:T(8,128)S(1)} %add_rsqrt_fusion.2, f32[16,256]{1,0:T(8,128)S(1)} %broadcast_multiply_fusion.2), kind=kOutput, calls=%fused_computation.106 | convolution fusion | flops 137097216 | bytes 6864896 | tf_op jit(solution)/shard_map/while/body/eval_jaxpr/qhd,hrd->hqr/dot_general | solution.py:40
  174.4 2.0 pad_maximum_fusion
  176.4 2.0 fusion.89
  178.4 3.7 %fusion.1 = f32[16,256]{1,0:T(8,128)S(1)} fusion(f32[16,256,256]{2,1,0:T(8,128)S(1)} %get-tuple-element.41, f32[16,256,768]{2,1,0:T(8,128)S(1)} %get-tuple-element.39, f32[16,256]{1,0:T(8,128)S(1)} %reduce_max.33), kind=kLoop, calls=%fused_computation.4 | loop fusion | flops 12578816 | bytes 16809984 | tf_op jit(solution)/shard_map/while/body/eval_jaxpr/reduce_sum | solution.py:43
  182.1 3.1 %divide_convert_fusion = bf16[16,256,1024]{2,1,0:T(8,128)(2,1)S(1)} fusion(f32[16,256,256]{2,1,0:T(8,128)S(1)} %get-tuple-element.41, f32[16,256,768]{2,1,0:T(8,128)S(1)} %get-tuple-element.39, f32[16,256]{1,0:T(8,128)S(1)} %fusion.1, f32[16,256]{1,0:T(8,128)S(1)} %reduce_max.33), kind=kLoop, calls=%fused_computation.2 | loop fusion | flops 16777216 | bytes 25198592 | tf_op jit(solution)/shard_map/while/body/eval_jaxpr/convert_element_type | solution.py:43
  185.2 4.1 %fusion.23 = f32[16,64,256]{2,1,0:T(8,128)S(1)} fusion(bf16[16,256,1024]{2,1,0:T(8,128)(2,1)S(1)} %divide_convert_fusion, f32[16,256,128]{2,1,0:T(8,128)S(1)} %convert_divide_fusion, f32[16,256]{1,0:T(8,128)S(1)} %add_rsqrt_fusion.1, f32[16,256]{1,0:T(8,128)S(1)} %broadcast_multiply_fusion.1), kind=kOutput, calls=%fused_computation.32 | convolution fusion | flops 135004160 | bytes 5275648 | tf_op jit(solution)/shard_map/while/body/eval_jaxpr/hqr,hrd->qhd/dot_general | solution.py:48
  189.4 2.1 fusion.45
  191.5 0.8 convert_reduce_fusion.1
  192.6 3.6 %all-gather.7.cloned.1.call-done = bf16[1024,4096]{1,0:T(8,128)(2,1)} async-done(((bf16[1024,512]{1,0:T(8,128)(2,1)}), bf16[1024,4096]{1,0:T(8,128)(2,1)}) %all-gather.7.cloned.1.call-update) | async-done | bytes 8388624 | tf_op jit(solution)/shard_map/all_gather | solution.py:109
  196.2 11.5 %fusion.54 = bf16[1,256,1024]{2,1,0:T(8,128)(2,1)} fusion(bf16[1024,4096]{1,0:T(8,128)(2,1)} %all-gather.11.cloned.1.call-done, bf16[256,1024]{1,0:T(8,128)(2,1)S(1)} %get-tuple-element.43, bf16[1024,4096]{1,0:T(8,128)(2,1)} %all-gather.7.cloned.1.call-done, f32[256]{0:T(256)S(1)} %add_rsqrt_fusion.3, f32[256]{0:T(256)S(1)} %broadcast_multiply_fusion.3), kind=kOutput, calls=%fused_computation.67 | convolution fusion | flops 4306239488 | bytes 17827840 | tf_op jit(solution)/shard_map/dot_general | solution.py:113
  (46 shorter events, 4.2 us)
Async XLA Ops:
  7.4 184.1 %copy-start = (bf16[1024,1024]{1,0:T(8,128)(2,1)S(1)}, bf16[1024,1024]{1,0:T(8,128)(2,1)}, u32[]{:S(2)}) copy-start(bf16[1024,1024]{1,0:T(8,128)(2,1)} %param.8) | copy-start | bytes 6291460
  7.4 51.7 %all-gather.9.cloned.1.call-start = ((), (), s32[]{:S(2)}) async-start(), calls=%async_computation.3 | async-start | bytes 1310720 | tf_op jit(solution)/shard_map/all_gather | solution.py:104
  8.1 61.3 %all-gather.5.cloned.1.call-start = ((), (), s32[]{:S(2)}) async-start(), calls=%async_computation.1 | async-start | bytes 1310720 | tf_op jit(solution)/shard_map/all_gather | solution.py:103
  8.8 154.7 %all-reduce.2.cloned.1.call-start = ((), (), s32[]{:S(2)}) async-start(), calls=%async_computation | async-start | bytes 2097152 | tf_op jit(solution)/shard_map/psum | solution.py:78
  51.6 4.4 %copy-start.1 = (f32[16,256,256]{2,1,0:T(8,128)S(1)}, f32[16,256,256]{2,1,0:T(8,128)}, u32[]{:S(2)}) copy-start(f32[16,256,256]{2,1,0:T(8,128)} %get-tuple-element.37) | copy-start | bytes 12582916
  51.6 4.4 %copy-start.2 = (bf16[256,16,64]{2,0,1:T(8,128)(2,1)S(1)}, bf16[256,16,64]{2,0,1:T(8,128)(2,1)}, u32[]{:S(2)}) copy-start(bf16[256,16,64]{2,0,1:T(8,128)(2,1)} %copy.25) | copy-start | bytes 1572868
  51.6 4.7 %copy-start.3 = (bf16[256,16,64]{2,0,1:T(8,128)(2,1)S(1)}, bf16[256,16,64]{2,0,1:T(8,128)(2,1)}, u32[]{:S(2)}) copy-start(bf16[256,16,64]{2,0,1:T(8,128)(2,1)} %copy.26) | copy-start | bytes 1572868
  59.0 133.6 %all-gather.11.cloned.1.call-start = ((), (), s32[]{:S(2)}) async-start(), calls=%async_computation.4 | async-start | bytes 9437184 | tf_op jit(solution)/shard_map/all_gather | solution.py:115
  59.7 136.5 %all-gather.7.cloned.1.call-start = ((), (), s32[]{:S(2)}) async-start(), calls=%async_computation.2 | async-start | bytes 9437184 | tf_op jit(solution)/shard_map/all_gather | solution.py:109
  71.6 102.7 %collective-permute-start = (bf16[256,2048]{0,1:T(8,128)(2,1)}, bf16[256,2048]{0,1:T(8,128)(2,1)}, u32[]{:S(2)}, u32[]{:S(2)}) collective-permute-start(bf16[256,2048]{0,1:T(8,128)(2,1)} %bitcast.3), channel_id=1, source_target_pairs={{0,1},{1,2},{2,3},{3,4},{4,5},{5,6},{6,7},{8,9},{9,10},{10,11},{11... | collective-permute-start | bytes 3145736 | tf_op jit(solution)/shard_map/ppermute | solution.py:20
  73.9 100.5 %collective-permute-start.1 = (bf16[256,2048]{0,1:T(8,128)(2,1)}, bf16[256,2048]{0,1:T(8,128)(2,1)}, u32[]{:S(2)}, u32[]{:S(2)}) collective-permute-start(bf16[256,2048]{0,1:T(8,128)(2,1)} %bitcast.3), channel_id=1, source_target_pairs={{1,0},{2,1},{3,2},{4,3},{5,4},{6,5},{7,6},{9,8},{10,9},{11,10},{12... | collective-permute-start | bytes 3145736 | tf_op jit(solution)/shard_map/ppermute | solution.py:21
  176.4 2.0 copy-start.4
  185.2 4.2 %copy-start.5 = (bf16[768,16,128]{0,2,1:T(8,128)(2,1)S(1)}, bf16[768,16,128]{0,2,1:T(8,128)(2,1)}, u32[]{:S(2)}) copy-start(bf16[768,16,128]{0,2,1:T(8,128)(2,1)} %copy-done.4) | copy-start | bytes 9437188
  189.4 2.1 copy-start.6
Sparse Core Ops, SparseCore 0:
  9.7 30.6 all-gather.8
  42.0 27.3 all-gather.4
  71.3 66.7 all-gather.10
  139.8 56.3 all-gather.6
Sparse Core Ops, SparseCore 1:
  59.1 104.4 all-reduce.1
where the time goes:
time: 215 us
  blocking collectives  69.7 us (32%)
  waiting for transfers between devices  55.8 us (26%)
  matrix products  40.5 us (19%)
  other arithmetic  22.3 us (10%)
  between operations  14.9 us (7%)
  local copies, waits for them, and re-layouts  8 us (4%)
  starting transfers between devices  3.7 us (2%)
    psum x1, blocking collectives, on_device(): lax.psum(totals.astype(jnp.bfloat16), 'seq').astype(jnp.float32)  43.4 us
    psum x1, waiting for transfers between devices, on_device(): lax.psum(sums.astype(jnp.bfloat16), 'seq').astype(jnp.float32)  40.4 us
    pmax x1, blocking collectives, on_device(): peaks = lax.pmax(peaks, 'seq')  26.3 us
    dot_general x1, matrix products, on_device(): lax.dot_general(hidden, lax.all_gather(down_part, 'seq', axis=1, tiled=Tr...  11.5 us
    all_gather x1, waiting for transfers between devices, on_device(): lax.all_gather(w_up, 'dp', axis=0, tiled=True)  9.67 us
    reduce_sum x4, other arithmetic, normalize(): spread = jnp.mean(center * center, axis=-1, keepdims=True)  4.91 us
    dot_general x1, matrix products, on_device(): jnp.dot(normed, w_qkv, preferred_element_type=jnp.float32)  4.86 us
    dot_general x1, matrix products, weighted_sums(): jnp.einsum('hnr,nhc->hrc', upper, paired, preferred_element_type=jnp.floa...  4.35 us
  transfers between devices with their start and end apart: 7, of which 3 were waited for; matrix products, arithmetic and copies ran while one was open for 27% of the time, Pallas kernels for 0%

commit v1 on v0

--- a/solution.py
+++ b/solution.py
@@ -73,9 +73,10 @@
     exponent = jnp.exp(logits - peaks[:, None, :])
     totals = jnp.sum(exponent, axis=1)
     sums = weighted_sums(exponent, paired)
+    _bind_circles = lambda panel, mesh_ax: jnp.sum(lax.all_gather(panel, mesh_ax), 0)
     totals, sums = (
         lax.psum(totals.astype(jnp.bfloat16), "seq").astype(jnp.float32),
-        lax.psum(sums.astype(jnp.bfloat16), "seq").astype(jnp.float32),
+        _bind_circles(sums.astype(jnp.bfloat16), mesh_ax="seq").astype(jnp.float32),
     )
     summary = sums / totals[..., None]
     far_keys = normalize(summary[..., :HS]).astype(jnp.bfloat16)

time: 215 us -> 269 us (1.25)
  waiting for transfers between devices: 55.8 us -> 98.9 us
  other arithmetic: 22.3 us -> 32.7 us
  blocking collectives: 69.7 us -> 65.1 us
  matrix products: 40.5 us -> 45 us
    all_gather x1, waiting for transfers between devices: 3.61 us -> 57.6 us  [on_device(): lax.all_gather(up_part, 'seq', axis=1, tiled=True)]
    psum x1 -> x0, waiting for transfers between devices: 40.4 us -> none  [on_device(): lax.psum(sums.astype(jnp.bfloat16), 'seq').astype(jnp.float32)]
    all_gather x1, waiting for transfers between devices: 0.02 us -> 22.1 us  [on_device(): lax.all_gather(down_part, 'seq', axis=1, tiled=True)]
    all_gather x0 -> x1, waiting for transfers between devices: none -> 7.37 us  [on_device(): lax.all_gather(panel, mesh_ax)]
    reduce_sum x0 -> x1, other arithmetic: none -> 6.14 us  [on_device(): jnp.sum(lax.all_gather(panel, mesh_ax), 0)]
    psum x1, blocking collectives: 43.4 us -> 38.7 us  [on_device(): lax.psum(totals.astype(jnp.bfloat16), 'seq').astype(jnp.float32)]
    dot_general x1, matrix products: 2.03 us -> 6.51 us  [attend(): jnp.einsum('qhd,khd->hqk', block_query, near_keys, preferred_element_type...]
    reduce_sum x1, other arithmetic: 3.7 us -> 8 us  [attend(): jax.nn.softmax(jnp.concatenate([near, far], axis=-1), axis=-1)]
  transfers between devices with their start and end apart: 7 -> 7, of which waited for: 3 -> 4; matrix products, arithmetic and copies ran while one was open for 27% -> 27% of each run, Pallas kernels for 0% -> 0%
where the time goes in v1:
time: 269 us; the launch traced here: 268 us
  waiting for transfers between devices  98.9 us (37%)
  blocking collectives  65.1 us (24%)
  matrix products  45 us (17%)
  other arithmetic  32.7 us (12%)
  between operations  13.5 us (5%)
  local copies, waits for them, and re-layouts  9.52 us (4%)
  starting transfers between devices  3.72 us (1%)
    all_gather x1, waiting for transfers between devices, on_device(): lax.all_gather(up_part, 'seq', axis=1, tiled=True)  57.6 us
    psum x1, blocking collectives, on_device(): lax.psum(totals.astype(jnp.bfloat16), 'seq').astype(jnp.float32)  38.7 us
    pmax x1, blocking collectives, on_device(): peaks = lax.pmax(peaks, 'seq')  26.3 us
    all_gather x1, waiting for transfers between devices, on_device(): lax.all_gather(down_part, 'seq', axis=1, tiled=True)  22.1 us
    dot_general x1, matrix products, on_device(): lax.dot_general(hidden, lax.all_gather(down_part, 'seq', axis=1, tiled=Tr...  11.5 us
    all_gather x1, waiting for transfers between devices, on_device(): lax.all_gather(w_up, 'dp', axis=0, tiled=True)  9.79 us
    reduce_sum x1, other arithmetic, attend(): jax.nn.softmax(jnp.concatenate([near, far], axis=-1), axis=-1)  8 us
    all_gather x1, waiting for transfers between devices, on_device(): lax.all_gather(panel, mesh_ax)  7.37 us
  transfers between devices with their start and end apart: 7, of which 4 were waited for; matrix products, arithmetic and copies ran while one was open for 27% of the time, Pallas kernels for 0%

profile of v1, /device:TPU:0, one launch (start us, length us, event | category | flops | bytes accessed | tf_op | source)
XLA Modules:
  0.0 268.4 jit_solution(6999489025287600214)
XLA Ops:
  8.1 1.2 convert_reduce_fusion.2
  9.3 1.3 fusion.59
  10.6 4.9 %convolution_convert_fusion = bf16[256,3072]{1,0:T(8,128)(2,1)S(1)} fusion(bf16[1024,3072]{1,0:T(8,128)(2,1)} %param.7, bf16[1,256,1024]{2,1,0:T(8,128)(2,1)} %param.6, f32[256]{0:T(256)S(1)} %add_rsqrt_fusion.4, f32[256]{0:T(256)S(1)} %broadcast_multiply_fusion.4), kind=kOutput, calls=%fused_computation.18 | convolution fusion | flops 1612447744 | bytes 8390656 | tf_op jit(solution)/shard_map/dot_general | solution.py:65
  16.8 1.2 copy.29
  18.0 1.4 copy.35
  19.4 1.3 copy.36
  20.7 3.7 %fusion.88 = (f32[16,256]{1,0:T(8,128)S(1)}, f32[16,256,256]{2,1,0:T(8,128)}) fusion(bf16[256,16,64]{0,2,1:T(8,128)(2,1)S(1)} %bitcast.44, bf16[16,64,256]{2,1,0:T(8,128)(2,1)} %param.9), kind=kOutput, calls=%fused_computation.104 | convolution fusion | flops 135262208 | bytes 5259264 | tf_op jit(solution)/shard_map/nhd,hdr->hnr/dot_general | solution.py:70
  24.4 26.3 %pmax.7 = f32[16,256]{1,0:T(8,128)S(1)} all-reduce(f32[16,256]{1,0:T(8,128)S(1)} %get-tuple-element.36), channel_id=1, replica_groups=mesh['dp'=4,'seq'=8] {'seq'}, use_global_device_ids=true, to_apply=%region_5.0 | all-reduce | flops 4096 | bytes 32768 | tf_op jit(solution)/shard_map/pmax | solution.py:72
  50.8 4.4 %fusion.14 = f32[16,256,128]{2,1,0:T(8,128)S(1)} fusion(f32[16,256,256]{2,1,0:T(8,128)} %get-tuple-element.37, f32[16,256]{1,0:T(8,128)S(1)} %pmax.7, bf16[256,16,64]{2,0,1:T(8,128)(2,1)} %copy.36, bf16[256,16,64]{2,0,1:T(8,128)(2,1)} %copy.35), kind=kOutput, calls=%fused_computation.22 | convolution fusion | flops 272629760 | bytes 7356416 | tf_op jit(solution)/shard_map/hnr,nhc->hrc/dot_general | solution.py:57
  55.4 2.7 %add_convert_fusion = bf16[16,256,128]{2,1,0:T(8,128)(2,1)} fusion(f32[16,256,128]{2,1,0:T(8,128)S(1)} %fusion.14, f32[16,256,256]{2,1,0:T(8,128)S(1)} %copy-done.1, f32[16,256]{1,0:T(8,128)S(1)} %pmax.7, bf16[256,16,64]{2,0,1:T(8,128)(2,1)S(1)} %copy-done.3, bf16[256,16,64]{2,0,1:T(8,128)(2,1)S(1)} %copy-done.2), kind=kOutput, calls=%fused_computation.43 | convolution fusion | flops 276824064 | bytes 8404992 | tf_op jit(solution)/shard_map/hnr,nhc->hrc/dot_general | solution.py:58
  58.8 9.8 %all-gather.7.cloned.1.call-done = bf16[1024,512]{1,0:T(8,128)(2,1)} async-done(((bf16[256,512]{1,0:T(8,128)(2,1)}), bf16[1024,512]{1,0:T(8,128)(2,1)}) %all-gather.7.cloned.1.call-update) | async-done | bytes 1048592 | tf_op jit(solution)/shard_map/all_gather | solution.py:104
  70.7 2.3 collective-permute-start
  73.0 1.3 collective-permute-start.1
  74.3 1.2 copy.32
  75.5 3.3 %fusion.12 = bf16[16,256]{1,0:T(8,128)(2,1)S(1)} fusion(f32[16,256,256]{2,1,0:T(8,128)} %get-tuple-element.37, f32[16,256]{1,0:T(8,128)S(1)} %pmax.7), kind=kLoop, calls=%fused_computation.19 | loop fusion | flops 2093056 | bytes 4218880 | tf_op jit(solution)/shard_map/reduce_sum | solution.py:74
  78.8 38.7 %psum.7 = bf16[16,256]{1,0:T(8,128)(2,1)S(1)} all-reduce(bf16[16,256]{1,0:T(8,128)(2,1)S(1)} %fusion.12), channel_id=1, replica_groups=mesh['dp'=4,'seq'=8] {'seq'}, use_global_device_ids=true, to_apply=%region_8.0 | all-reduce | flops 4096 | bytes 16384 | tf_op jit(solution)/shard_map/psum | solution.py:78
  117.6 2.0 pad_maximum_fusion
  119.6 1.6 copy-done.4
  121.2 6.5 %fusion.89 = (f32[16,256]{1,0:T(8,128)S(1)}, f32[16,256,768]{2,1,0:T(8,128)}) fusion(bf16[256,16,64]{0,2,1:T(8,128)(2,1)S(1)} %bitcast.53, bf16[768,16,128]{0,2,1:T(8,128)(2,1)S(1)} %pad_maximum_fusion, pred[768]{0:T(1024)(128)(4,1)S(1)} %fusion.80), kind=kOutput, calls=%fused_computation.105 | convolution fusion | flops 412086272 | bytes 14697472 | tf_op jit(solution)/shard_map/while/body/eval_jaxpr/qhd,khd->hqk/dot_general | solution.py:35
  127.7 7.4 %all-gather.15.cloned.1.call-done = bf16[128,256,128]{2,1,0:T(8,128)(2,1)} async-done(((bf16[16,256,128]{2,1,0:T(8,128)(2,1)}), bf16[128,256,128]{2,1,0:T(8,128)(2,1)}) %all-gather.15.cloned.1.call-update) | async-done | bytes 8388624 | tf_op jit(solution)/shard_map/all_gather | solution.py:76
  135.1 6.1 %reduce_sum.125 = bf16[16,256,128]{2,1,0:T(8,128)(2,1)} reduce(bf16[8,16,256,128]{3,2,1,0:T(8,128)(2,1)} %bitcast.52, bf16[]{:T(256)} %constant.64.clone.1), dimensions={0}, to_apply=%region_6.0 | reduce | flops 3670016 | bytes 9437186 | tf_op jit(solution)/shard_map/reduce_sum | solution.py:76
  141.2 1.8 convert_divide_fusion
  143.0 1.7 slice_reduce_fusion
  144.8 2.9 %multiply_reduce_fusion = (f32[16,256]{1,0:T(8,128)S(1)}, f32[16,256]{1,0:T(8,128)S(1)}) fusion(f32[16,256,128]{2,1,0:T(8,128)S(1)} %convert_divide_fusion, f32[16,256]{1,0:T(8,128)S(1)} %broadcast_multiply_fusion.1, f32[16,256]{1,0:T(8,128)S(1)} %broadcast_multiply_fusion.2), kind=kLoop, calls=%fused_computation.39 | loop fusion | flops 1564672 | bytes 2162688 | tf_op jit(solution)/shard_map/reduce_sum | solution.py:28
  147.7 4.3 %fusion.90 = (f32[16,256]{1,0:T(8,128)S(1)}, f32[16,256,256]{2,1,0:T(8,128)S(1)}) fusion(bf16[256,16,64]{0,2,1:T(8,128)(2,1)S(1)} %bitcast.54, f32[16,256,128]{2,1,0:T(8,128)S(1)} %convert_divide_fusion, f32[16,256]{1,0:T(8,128)S(1)} %add_rsqrt_fusion.2, f32[16,256]{1,0:T(8,128)S(1)} %broadcast_multiply_fusion.2), kind=kOutput, calls=%fused_computation.106 | convolution fusion | flops 137097216 | bytes 6864896 | tf_op jit(solution)/shard_map/while/body/eval_jaxpr/qhd,hrd->hqr/dot_general | solution.py:40
  152.1 8.0 %fusion.1 = f32[16,256]{1,0:T(8,128)S(1)} fusion(f32[16,256,256]{2,1,0:T(8,128)S(1)} %get-tuple-element.41, f32[16,256,768]{2,1,0:T(8,128)} %get-tuple-element.39, f32[16,256]{1,0:T(8,128)S(1)} %reduce_max.33), kind=kLoop, calls=%fused_computation.4 | loop fusion | flops 12578816 | bytes 16809984 | tf_op jit(solution)/shard_map/while/body/eval_jaxpr/reduce_sum | solution.py:43
  160.2 3.1 %divide_convert_fusion = bf16[16,256,1024]{2,1,0:T(8,128)(2,1)S(1)} fusion(f32[16,256,256]{2,1,0:T(8,128)S(1)} %get-tuple-element.41, f32[16,256,768]{2,1,0:T(8,128)S(1)} %bitcast.42, f32[16,256]{1,0:T(8,128)S(1)} %fusion.1, f32[16,256]{1,0:T(8,128)S(1)} %reduce_max.33), kind=kLoop, calls=%fused_computation.2 | loop fusion | flops 16777216 | bytes 25198592 | tf_op jit(solution)/shard_map/while/body/eval_jaxpr/convert_element_type | solution.py:43
  163.2 4.1 %fusion.23 = f32[16,64,256]{2,1,0:T(8,128)S(1)} fusion(bf16[16,256,1024]{2,1,0:T(8,128)(2,1)S(1)} %divide_convert_fusion, f32[16,256,128]{2,1,0:T(8,128)S(1)} %convert_divide_fusion, f32[16,256]{1,0:T(8,128)S(1)} %add_rsqrt_fusion.1, f32[16,256]{1,0:T(8,128)S(1)} %broadcast_multiply_fusion.1), kind=kOutput, calls=%fused_computation.32 | convolution fusion | flops 135004160 | bytes 5275648 | tf_op jit(solution)/shard_map/while/body/eval_jaxpr/hqr,hrd->qhd/dot_general | solution.py:48
  167.4 2.0 fusion.45
  170.6 22.1 %all-gather.13.cloned.1.call-done = bf16[1024,4096]{1,0:T(8,128)(2,1)} async-done(((bf16[1024,512]{1,0:T(8,128)(2,1)}), bf16[1024,4096]{1,0:T(8,128)(2,1)}) %all-gather.13.cloned.1.call-update) | async-done | bytes 8388624 | tf_op jit(solution)/shard_map/all_gather | solution.py:116
  192.7 57.6 %all-gather.9.cloned.1.call-done = bf16[1024,4096]{1,0:T(8,128)(2,1)} async-done(((bf16[1024,512]{1,0:T(8,128)(2,1)}), bf16[1024,4096]{1,0:T(8,128)(2,1)}) %all-gather.9.cloned.1.call-update) | async-done | bytes 8388624 | tf_op jit(solution)/shard_map/all_gather | solution.py:110
  250.3 11.5 %fusion.54 = bf16[1,256,1024]{2,1,0:T(8,128)(2,1)} fusion(bf16[1024,4096]{1,0:T(8,128)(2,1)} %all-gather.13.cloned.1.call-done, bf16[256,1024]{1,0:T(8,128)(2,1)S(1)} %get-tuple-element.43, bf16[1024,4096]{1,0:T(8,128)(2,1)} %all-gather.9.cloned.1.call-done, f32[256]{0:T(256)S(1)} %add_rsqrt_fusion.3, f32[256]{0:T(256)S(1)} %broadcast_multiply_fusion.3), kind=kOutput, calls=%fused_computation.67 | convolution fusion | flops 4306239488 | bytes 17827840 | tf_op jit(solution)/shard_map/dot_general | solution.py:114
  (54 shorter events, 7.0 us)
Async XLA Ops:
  6.5 162.9 %copy-start = (bf16[1024,1024]{1,0:T(8,128)(2,1)S(1)}, bf16[1024,1024]{1,0:T(8,128)(2,1)}, u32[]{:S(2)}) copy-start(bf16[1024,1024]{1,0:T(8,128)(2,1)} %param.8) | copy-start | bytes 6291460
  6.5 51.7 %all-gather.11.cloned.1.call-start = ((), (), s32[]{:S(2)}) async-start(), calls=%async_computation.2 | async-start | bytes 1310720 | tf_op jit(solution)/shard_map/all_gather | solution.py:105
  7.3 61.3 %all-gather.7.cloned.1.call-start = ((), (), s32[]{:S(2)}) async-start(), calls=%async_computation | async-start | bytes 1310720 | tf_op jit(solution)/shard_map/all_gather | solution.py:104
  8.0 127.1 %all-gather.15.cloned.1.call-start = ((), (), s32[]{:S(2)}) async-start(), calls=%async_computation.4 | async-start | bytes 9437184 | tf_op jit(solution)/shard_map/all_gather | solution.py:76
  50.8 4.4 %copy-start.1 = (f32[16,256,256]{2,1,0:T(8,128)S(1)}, f32[16,256,256]{2,1,0:T(8,128)}, u32[]{:S(2)}) copy-start(f32[16,256,256]{2,1,0:T(8,128)} %get-tuple-element.37) | copy-start | bytes 12582916
  50.8 4.4 %copy-start.2 = (bf16[256,16,64]{2,0,1:T(8,128)(2,1)S(1)}, bf16[256,16,64]{2,0,1:T(8,128)(2,1)}, u32[]{:S(2)}) copy-start(bf16[256,16,64]{2,0,1:T(8,128)(2,1)} %copy.35) | copy-start | bytes 1572868
  50.8 4.7 %copy-start.3 = (bf16[256,16,64]{2,0,1:T(8,128)(2,1)S(1)}, bf16[256,16,64]{2,0,1:T(8,128)(2,1)}, u32[]{:S(2)}) copy-start(bf16[256,16,64]{2,0,1:T(8,128)(2,1)} %copy.36) | copy-start | bytes 1572868
  58.2 134.5 %all-gather.13.cloned.1.call-start = ((), (), s32[]{:S(2)}) async-start(), calls=%async_computation.3 | async-start | bytes 9437184 | tf_op jit(solution)/shard_map/all_gather | solution.py:116
  58.8 191.6 %all-gather.9.cloned.1.call-start = ((), (), s32[]{:S(2)}) async-start(), calls=%async_computation.1 | async-start | bytes 9437184 | tf_op jit(solution)/shard_map/all_gather | solution.py:110
  70.7 46.9 %collective-permute-start = (bf16[256,2048]{0,1:T(8,128)(2,1)}, bf16[256,2048]{0,1:T(8,128)(2,1)}, u32[]{:S(2)}, u32[]{:S(2)}) collective-permute-start(bf16[256,2048]{0,1:T(8,128)(2,1)} %bitcast.3), channel_id=1, source_target_pairs={{0,1},{1,2},{2,3},{3,4},{4,5},{5,6},{6,7},{8,9},{9,10},{10,11},{11... | collective-permute-start | bytes 3145736 | tf_op jit(solution)/shard_map/ppermute | solution.py:20
  73.0 44.6 %collective-permute-start.1 = (bf16[256,2048]{0,1:T(8,128)(2,1)}, bf16[256,2048]{0,1:T(8,128)(2,1)}, u32[]{:S(2)}, u32[]{:S(2)}) collective-permute-start(bf16[256,2048]{0,1:T(8,128)(2,1)} %bitcast.3), channel_id=1, source_target_pairs={{1,0},{2,1},{3,2},{4,3},{5,4},{6,5},{7,6},{9,8},{10,9},{11,10},{12... | collective-permute-start | bytes 3145736 | tf_op jit(solution)/shard_map/ppermute | solution.py:21
  119.6 1.6 copy-start.4
  147.7 12.4 %slice-start = ((s8[12582912]{0:T(1024)(128)(4,1)}), s8[4194304]{0:T(1024)(128)(4,1)S(1)}, s32[]{:S(2)}) async-start(s8[12582912]{0:T(1024)(128)(4,1)} %bitcast.41), calls=%async_computation.5 | async-start | bytes 8388608
  152.1 8.0 %slice-start.1 = ((s8[12582912]{0:T(1024)(128)(4,1)}), s8[4194304]{0:T(1024)(128)(4,1)S(1)}, s32[]{:S(2)}) async-start(s8[12582912]{0:T(1024)(128)(4,1)} %bitcast.41), calls=%async_computation.6 | async-start | bytes 8388608
  152.1 8.0 %slice-start.2 = ((s8[12582912]{0:T(1024)(128)(4,1)}), s8[4194304]{0:T(1024)(128)(4,1)S(1)}, s32[]{:S(2)}) async-start(s8[12582912]{0:T(1024)(128)(4,1)} %bitcast.41), calls=%async_computation.7 | async-start | bytes 8388608
  163.2 4.2 %copy-start.5 = (bf16[768,16,128]{0,2,1:T(8,128)(2,1)S(1)}, bf16[768,16,128]{0,2,1:T(8,128)(2,1)}, u32[]{:S(2)}) copy-start(bf16[768,16,128]{0,2,1:T(8,128)(2,1)} %copy-done.4) | copy-start | bytes 9437188
  167.4 2.0 copy-start.6
Sparse Core Ops, SparseCore 0:
  8.9 30.6 all-gather.10
  41.2 27.3 all-gather.6
  70.5 64.5 all-gather.14
  136.8 55.8 all-gather.12
  194.4 55.8 all-gather.8
